TPU v7x, 32 devices: a whole 2x2x4 slice. The times are simulated.
32 devices in a mesh: child: 2 (over x), row: 4 (over z), col: 4 (over y, core).
Axes of the slice: x: 2, y: 2, z: 4, core: 2. Of those that a mesh axis runs over, the one named last changes fastest.
Arguments:
- contrib: float32 [2, 2048, 2048], P('child', 'row', 'col'), may hold values from -0.125 to 0.125
- assembled: float32 [2, 2048, 4096], P('child', 'row', 'col'), may hold values from -0.125 to 0.125
- pattern: int32 [16, 16], P('row', 'col'), may hold values 0 or 1
- omega: float32 [4096, 256], P('col', 'row'), may hold values from -6 to 6
- row_maps: int32 [2, 2048], P('child'), may hold values from 0 to 4095, as said below
- leaf_bounds: int32 [4], P('row'), may hold values from 448 to 576
Outputs:
- bases: float32 [4096, 256], P('row', ('child', 'col'))
- coupling: float32 [4, 2, 256, 256], P('row', None, ('child', 'col'))
Inputs may be any that keep to these rules, and one draw needn't show every extreme that they name: `row_maps`: for each child, entries k * 512 to (k + 1) * 512 - 1 are distinct, rising, and lie in k * 1024 to (k + 1) * 1024 - 1.
All inputs are finite; a program needn't handle non-finite values. No bound on the sum of `pattern` on one device may be relied on, other than what follows from the above.
Results may differ from a plain program's by a relative error of at most 0.0003.
Values sent between devices are 32-bit elements; how exact they have to be, the bound alone decides.
A program may use at most 64 MiB of HBM per device.

v0:
```python
import jax
import jax.numpy as jnp
from jax import lax
from jax.experimental import pallas as pl
from jax.experimental.pallas import tpu as pltpu
from jax.sharding import PartitionSpec as P

BT = 256
NB = 64
SUB = 8
MESH = pl.DeviceIdType.MESH
VMEM = pl.BlockSpec(memory_space=pltpu.VMEM)
SMEM = pl.BlockSpec(memory_space=pltpu.SMEM)

NN = (((1,), (0,)), ((), ()))
NT = (((1,), (1,)), ((), ()))
TN = (((0,), (0,)), ((), ()))


def split(a):
    high = a.astype(jnp.bfloat16)
    low = (a - high.astype(jnp.float32)).astype(jnp.bfloat16)
    return high, low


def dot16(a, b, dims=NN):
    return lax.dot_general(a, b, dims, preferred_element_type=jnp.float32)


def mm3(a, b, dims=NN):
    (ah, al), (bh, bl) = split(a), split(b)
    return dot16(ah, bh, dims) + (dot16(ah, bl, dims) + dot16(al, bh, dims))


class Plane:
    def __init__(self):
        self.cols = lax.axis_size("col")
        self.chips = self.cols * lax.axis_size("child") // 2
        self.group = lax.axis_index("child") * self.cols + lax.axis_index("col")
        self.chip = self.group // 2
        self.core = self.group % 2
        self.order = [lax.rem(self.chip + step, self.chips) for step in range(self.chips)]

    def device(self, chip, core):
        flat = chip * 2 + core
        return {"child": flat // self.cols, "col": flat % self.cols}


def remote(source, target, send_sem, recv_sem, device):
    return pltpu.make_async_remote_copy(
        src_ref=source, dst_ref=target, send_sem=send_sem, recv_sem=recv_sem, device_id=device, device_id_type=MESH
    )


def greet(plane):
    count = lax.axis_size("row")
    me = lax.axis_index("row")
    barrier = pltpu.get_barrier_semaphore()

    @pl.when(me > 0)
    def _():
        pl.semaphore_signal(barrier, inc=1, device_id={"row": me - 1}, device_id_type=MESH)

    @pl.when(me < count - 1)
    def _():
        pl.semaphore_signal(barrier, inc=1, device_id={"row": me + 1}, device_id_type=MESH)

    pl.semaphore_signal(barrier, inc=1, device_id=plane.device(plane.chip, 1 - plane.core), device_id_type=MESH)
    for step in range(1, plane.chips):
        pl.semaphore_signal(
            barrier, inc=1, device_id=plane.device(plane.order[step], plane.core), device_id_type=MESH
        )
    pl.semaphore_wait(barrier, plane.chips + jnp.minimum(me, 1) + jnp.minimum(count - 1 - me, 1))


def gather(own_ref, out_ref, sems, prepare, stage, settle, finalize):
    send_right, send_left, recv, swap_send, swap_recv, local_sem = sems
    count = lax.axis_size("row")
    me = lax.axis_index("row")
    half = lax.axis_index("child")
    has_left = me > 0
    has_right = me < count - 1
    keep = pltpu.make_async_copy(own_ref, out_ref.at[me], local_sem)
    keep.start()

    def hop(block, target, step, send):
        source = own_ref.at[half] if step == 0 else out_ref.at[block, half]
        return remote(source, out_ref.at[block, half], send.at[block], recv.at[block], {"row": target})

    def swap(block):
        place = out_ref.at[block, half]
        return remote(place, place, swap_send.at[block], swap_recv.at[block], {"child": 1 - half})

    def at_distance(step, act):
        for block, there in ((me - step, me >= step), (me + step, me + step < count)):

            @pl.when(there)
            def _():
                act(block)

    def wait_swap(block):
        place = out_ref.at[block, 1 - half]
        remote(place, place, swap_send.at[block], swap_recv.at[block], {"child": 1 - half}).wait_recv()

    def staged(block):
        wait_swap(block)
        stage(block)

    for step in range(count):
        low = me - step
        high = me + step
        if step > 0:

            @pl.when(low >= 0)
            def _():
                hop(low, me - 1, step, send_right).wait_recv()

        @pl.when(jnp.logical_and(low >= 0, has_right))
        def _():
            hop(low, me + 1, step, send_right).start()

        if step > 0:

            @pl.when(low >= 0)
            def _():
                swap(low).start()

            @pl.when(high < count)
            def _():
                hop(high, me + 1, step, send_left).wait_recv()

        @pl.when(jnp.logical_and(high < count, has_left))
        def _():
            hop(high, me - 1, step, send_left).start()

        if step > 0:

            @pl.when(high < count)
            def _():
                swap(high).start()

        if step == 0:
            prepare()
            keep.wait()
            stage(me)
        else:
            if step > 1:
                at_distance(step - 1, staged)
            if step == 2:
                settle(me)
            if step > 2:
                at_distance(step - 2, settle)
            if step == 3:
                finalize(me)
            if step > 3:
                at_distance(step - 3, finalize)
    at_distance(count - 1, staged)
    if count == 2:
        settle(me)
    if count > 2:
        at_distance(count - 2, settle)
    if count < 4:
        finalize(me)
    for step in range(max(count - 3, 1), count - 1):
        at_distance(step, finalize)
    at_distance(count - 1, settle)
    at_distance(count - 1, finalize)

    def drain():
        for step in range(count):
            low = me - step
            high = me + step

            @pl.when(jnp.logical_and(low >= 0, has_right))
            def _():
                hop(low, me + 1, step, send_right).wait_send()

            @pl.when(jnp.logical_and(high < count, has_left))
            def _():
                hop(high, me - 1, step, send_left).wait_send()

        for step in range(1, count):
            swap(lax.rem(me + step, count)).wait_send()

    def nearest(act):
        act(me)
        for step in range(1, count):
            at_distance(step, act)

    return drain, nearest


def prepare_sketch(pattern_ref, contrib, assembled, maps_ref, held):
    pick, place, front, entries = held
    half = lax.axis_index("child")
    tile_rows, tile_cols = contrib.shape
    window_rows = assembled.shape[1]
    row_pos, col_pos = lax.axis_index("row"), lax.axis_index("col")
    columns = maps_ref[:, pl.ds(pl.multiple_of(col_pos * tile_cols, tile_cols), tile_cols)] - col_pos * window_rows
    targets = maps_ref[:, pl.ds(pl.multiple_of(row_pos * tile_rows, tile_rows), tile_rows)] - row_pos * window_rows
    index = lax.broadcasted_iota(jnp.int32, (window_rows, tile_cols), 0)
    pick[...] = jnp.where(index == columns, 1.0, 0.0).astype(jnp.bfloat16)
    index = lax.broadcasted_iota(jnp.int32, (window_rows, tile_rows), 0)
    place[...] = jnp.where(index == targets, 1.0, 0.0).astype(jnp.bfloat16)
    front[0], front[1] = split(contrib[...])
    for row in range(tile_rows // BT):
        for col in range(window_rows // BT):
            where = (slice(row * BT, (row + 1) * BT), slice(col * BT, (col + 1) * BT))
            present = pattern_ref[half * (tile_rows // BT) + row, col].astype(jnp.float32)
            entries[(0,) + where], entries[(1,) + where] = split(assembled[where] * present)


def stacked(a, b, dims=NN):
    rows = a.shape[0] // 2
    both = dot16(a, b[0], dims)
    return both[:rows] + (dot16(a[:rows], b[1], dims) + both[rows:])


def sketch(omega, held, part_ref):
    pick, place, front, entries = held
    half = lax.axis_index("child")
    rows, tile_rows = omega.shape[0], place.shape[1]
    both = jnp.concatenate(split(omega), axis=0)
    picked = dot16(both, pick[...]).astype(jnp.bfloat16)
    product = stacked(picked, front, NT)
    sparse = stacked(both, entries, NT)
    spread = dot16(jnp.concatenate(split(product), axis=0), place[...], NT)
    part_ref[...] = (spread[:rows] + spread[rows:]).reshape(part_ref.shape)
    where = pl.ds(pl.multiple_of(half * tile_rows, tile_rows), tile_rows)
    part_ref[:, :, :, where] = part_ref[:, :, :, where] + sparse.reshape(part_ref.shape[:3] + (tile_rows,))


class Reduce:
    def __init__(self, plane, part_ref, out_ref, pair_buf, sum_buf, chip_buf, sems):
        self.plane, self.part, self.out = plane, part_ref, out_ref
        self.pair_buf, self.sum_buf, self.chip_buf, self.sems = pair_buf, sum_buf, chip_buf, sems
        self.partner = plane.device(plane.chip, 1 - plane.core)

    def pair(self, r):
        source = self.part.at[r, :, 1 - self.plane.core]
        return remote(source, self.pair_buf.at[r], self.sems[0].at[r], self.sems[1].at[r], self.partner)

    def give(self, r, c):
        chip = self.plane.chip
        device = self.plane.device(c, self.plane.core)
        return remote(
            self.sum_buf.at[r, c], self.chip_buf.at[r, chip], self.sems[2].at[r, c], self.sems[3].at[r, chip], device
        )

    def take(self, r, c):
        device = self.plane.device(c, self.plane.core)
        return remote(self.sum_buf.at[r, c], self.chip_buf.at[r, c], self.sems[2].at[r, c], self.sems[3].at[r, c], device)

    def show(self, r, c, owner):
        block = self.out.at[r, owner, self.plane.core]
        device = self.plane.device(c, self.plane.core)
        return remote(block, block, self.sems[4].at[r, c], self.sems[5].at[r, owner], device)

    def hand(self, r, c, core):
        block = self.out.at[r, c, core]
        return remote(block, block, self.sems[6].at[r, c], self.sems[7].at[r, c], self.partner)

    def begin(self, r):
        self.pair(r).start()

    def settle(self, r):
        plane = self.plane
        self.pair(r).wait_recv()
        for c in plane.order[1:]:
            self.sum_buf[r, c] = self.part[r, c, plane.core] + self.pair_buf[r, c]
            self.give(r, c).start()

    def finalize(self, r):
        plane = self.plane
        chip, core, others = plane.chip, plane.core, plane.order[1:]
        total = self.part[r, chip, core] + self.pair_buf[r, chip]
        for c in others:
            self.take(r, c).wait_recv()
            total = total + self.chip_buf[r, c]
        self.out[r, chip, core] = total
        for c in others:
            self.show(r, c, chip).start()
        self.hand(r, chip, core).start()

    def forward(self, r):
        for c in self.plane.order[1:]:
            self.show(r, c, c).wait_recv()
            self.hand(r, c, self.plane.core).start()

    def arrive(self, r):
        for c in self.plane.order:
            self.hand(r, c, 1 - self.plane.core).wait_recv()

    def drain(self, stages):
        for r in stages:
            self.pair(r).wait_send()
            for c in self.plane.order[1:]:
                self.give(r, c).wait_send()
                self.show(r, c, self.plane.chip).wait_send()
            for c in self.plane.order:
                self.hand(r, c, self.plane.core).wait_send()


def eliminate(leaves):
    groups = NB // SUB
    index = lax.broadcasted_iota(jnp.int32, (SUB, 2 * NB), 0)
    wide = (SUB, 2 * NB)
    leaves = [list(rows) for rows in leaves]
    for panel in range(groups):
        first = panel * SUB
        columns = [
            {
                q: [jnp.broadcast_to(rows[q][:, first + k : first + k + 1], wide) for k in range(SUB)]
                for q in range(panel, groups)
            }
            for rows in leaves
        ]
        for k in range(SUB):
            for rows, cols in zip(leaves, columns):
                own = cols[panel]
                scale = lax.rsqrt(jnp.broadcast_to(own[k][k : k + 1], wide))
                pivot = jnp.broadcast_to(rows[panel][k : k + 1], wide) * scale
                weight = {q: cols[q][k] * scale for q in range(panel, groups)}
                across = weight[panel]
                below = jnp.where(index > k, across, 0.0)
                rows[panel] = jnp.where(index == k, pivot, rows[panel] - below * pivot)
                for j in range(k + 1, SUB):
                    factor = jnp.broadcast_to(across[j : j + 1], wide)
                    for q in range(panel, groups):
                        cols[q][j] = cols[q][j] - (below if q == panel else weight[q]) * factor
                for q in range(panel + 1, groups):
                    rows[q] = rows[q] - weight[q] * pivot
    return leaves


def factor(bound, window, work, done_block):
    columns, window_rows = window.shape
    top = window_rows // 2 + window_rows // 16
    low = window_rows // 2 - window_rows // 16
    eye = jnp.where(
        lax.broadcasted_iota(jnp.int32, (columns, columns), 0)
        == lax.broadcasted_iota(jnp.int32, (columns, columns), 1),
        1.0,
        0.0,
    )
    lane = lax.broadcasted_iota(jnp.int32, (columns, window_rows), 1)
    head = jnp.where(lane < bound, window, 0.0)
    tail = window - head
    spans = ((head, 0, (top + 127) // 128 * 128), (tail, low // 128 * 128, window_rows))
    counts = (bound, window_rows - bound)
    for leaf, (masked, start, stop) in enumerate(spans):
        part = masked[:, start:stop]
        gram = mm3(part, part, NT)
        work[leaf, :, :columns] = gram / counts[leaf].astype(jnp.float32)
        work[leaf, :, columns:] = eye
    small_eye = eye[:NB, :NB]
    for block in range(columns // NB):
        begin, end = block * NB, (block + 1) * NB
        aug = []
        for leaf in range(2):
            diagonal = jnp.concatenate([work[leaf, begin:end, begin:end], small_eye], axis=1)
            aug.append([diagonal[q * SUB : (q + 1) * SUB] for q in range(NB // SUB)])
        done = eliminate(aug)
        for leaf in range(2):
            inverse = jnp.concatenate(done[leaf], axis=0)[:, NB:]
            rows = mm3(inverse, work[leaf, begin:end, :])
            work[leaf, begin:end, :] = rows
            done_block(leaf, block, begin, end, rows[:, :columns])
            if end < columns:
                work[leaf, end:, :] = work[leaf, end:, :] - mm3(rows[:, end:columns], rows, TN)


def whole_kernel(
    bound_ref, pattern_ref, omega_ref, contrib_ref, assembled_ref, maps_ref, bases_ref, coupling_ref,
    gathered, contrib_buf, assembled_buf, pick, place, front, entries,
    part, window, pair_buf, sum_buf, chip_buf, work, upper, sibling, input_sems, *sems,
):
    plane = Plane()
    window_rows = assembled_buf.shape[1]
    columns, width = upper.shape[1], bases_ref.shape[0]
    held = (pick, place, front, entries)
    load_front = pltpu.make_async_copy(contrib_ref.at[0], contrib_buf, input_sems.at[0])
    load_entries = pltpu.make_async_copy(assembled_ref.at[0], assembled_buf, input_sems.at[1])
    load_front.start()
    load_entries.start()
    greet(plane)

    def prepare():
        load_front.wait()
        load_entries.wait()
        prepare_sketch(pattern_ref, contrib_buf, assembled_buf, maps_ref, held)

    stages = part.shape[0]
    row_count, row_pos = lax.axis_size("row"), lax.axis_index("row")
    summing = Reduce(plane, part, window, pair_buf, sum_buf, chip_buf, sems[6:14])
    if stages == row_count:

        def stage(block):
            sketch(gathered[block].reshape(columns // stages, window_rows), held, part.at[block])
            summing.begin(block)

        drain_gather, nearest = gather(
            omega_ref, gathered, sems[:6], prepare, stage, summing.settle, lambda block: None
        )
        nearest(summing.finalize)
        nearest(summing.forward)
        order = [lax.rem(row_pos + step, row_count) for step in range(row_count)]
    else:
        idle = lambda block: None
        drain_gather, nearest = gather(omega_ref, gathered, sems[:6], prepare, idle, idle, idle)
        sketch(gathered[...].reshape(columns, window_rows), held, part.at[0])
        summing.begin(0)
        summing.settle(0)
        summing.finalize(0)
        summing.forward(0)
        order = [0]
    for r in order:
        summing.arrive(r)
    drain_gather()
    summing.drain(order)

    near_send, near_recv = sems[14:]
    near = {"row": row_pos + 1 - 2 * (row_pos % 2)}

    def send(leaf, block):
        start = block * NB // 128 * 128
        rows = slice(block * NB, (block + 1) * NB)
        source, target = upper.at[leaf, rows, start:], sibling.at[leaf, rows, start:]
        return remote(source, target, near_send.at[leaf, block], near_recv.at[leaf, block], near)

    def done_block(leaf, block, begin, end, rows):
        keep = lax.broadcasted_iota(jnp.int32, rows.shape, 1) >= begin + lax.broadcasted_iota(
            jnp.int32, rows.shape, 0
        )
        upper[leaf, begin:end, :] = jnp.where(keep, rows, 0.0)
        send(leaf, block).start()

    bound = bound_ref[0]
    samples = window[...].reshape(columns, window_rows)
    factor(bound, samples, work, done_block)
    mine = pl.ds(pl.multiple_of(plane.group * width, width), width)
    inverse = jnp.concatenate([work[0, mine, columns:], work[1, mine, columns:]], axis=0)
    both = mm3(inverse, samples)
    lane = lax.broadcasted_iota(jnp.int32, (width, window_rows), 1)
    bases_ref[...] = jnp.where(lane < bound, both[:width], both[width:])
    for leaf in range(2):
        own = upper[leaf, mine, :]
        pieces = []
        for block in range(columns // NB):
            start = block * NB // 128 * 128
            send(leaf, block).wait_recv()
            pieces.append(mm3(own[:, start:], sibling[leaf, block * NB : (block + 1) * NB, start:], NT))
        coupling_ref[0, leaf] = jnp.concatenate(pieces, axis=1)
    for leaf in range(2):
        for block in range(columns // NB):
            send(leaf, block).wait_send()


def deliver_kernel(bases_ref, coupling_ref, bases_out, coupling_out):
    bases_out[...] = bases_ref[...]
    coupling_out[...] = coupling_ref[...]


def local(contrib, assembled, pattern, omega, row_maps, leaf_bounds):
    tile_rows, tile_cols = contrib.shape[1:]
    window_rows, own_width = omega.shape
    rows = lax.axis_size("row")
    chips = lax.axis_size("col") * lax.axis_size("child") // 2
    columns = own_width * rows
    width = columns // (2 * chips)
    own = omega.T.reshape(2, own_width // 2, window_rows)
    f32, bf16, dma = jnp.float32, jnp.bfloat16, pltpu.SemaphoreType.DMA
    any_space = pl.BlockSpec(memory_space=pl.ANY)
    stages = rows if columns // (rows * 2 * chips) >= SUB else 1
    piece = width // stages
    block = pltpu.VMEM((stages, chips, piece, window_rows), f32)
    split_window = pltpu.VMEM((stages, chips, 2, piece, window_rows), f32)
    bases, coupling = pl.pallas_call(
        whole_kernel,
        out_shape=(
            jax.ShapeDtypeStruct((width, window_rows), f32),
            jax.ShapeDtypeStruct((1, 2, width, columns), f32),
        ),
        in_specs=[SMEM, SMEM, VMEM, any_space, any_space, VMEM],
        out_specs=(VMEM, VMEM),
        scratch_shapes=[
            pltpu.VMEM((rows, 2, own_width // 2, window_rows), f32),
            pltpu.VMEM((tile_rows, tile_cols), f32),
            pltpu.VMEM((tile_rows, window_rows), f32),
            pltpu.VMEM((window_rows, tile_cols), bf16),
            pltpu.VMEM((window_rows, tile_rows), bf16),
            pltpu.VMEM((2, tile_rows, tile_cols), bf16),
            pltpu.VMEM((2, tile_rows, window_rows), bf16),
            split_window,
            split_window,
            block,
            block,
            block,
            pltpu.VMEM((2, columns, 2 * columns), f32),
            pltpu.VMEM((2, columns, columns), f32),
            pltpu.VMEM((2, columns, columns), f32),
            dma((2,)),
        ]
        + [dma((rows,))] * 5
        + [dma]
        + [dma((stages,))] * 2
        + [dma((stages, chips))] * 6
        + [dma((2, columns // NB))] * 2,
        compiler_params=pltpu.CompilerParams(
            collective_id=0, has_side_effects=True, vmem_limit_bytes=56 << 20
        ),
        name="front_samples",
    )(leaf_bounds, pattern, own, contrib, assembled, row_maps)
    bases, coupling = pl.pallas_call(
        deliver_kernel,
        out_shape=(
            jax.ShapeDtypeStruct(bases.shape, f32),
            jax.ShapeDtypeStruct(coupling.shape, f32),
        ),
        in_specs=[VMEM, VMEM],
        out_specs=(VMEM, VMEM),
        name="deliver",
    )(bases, coupling)
    return (bases.T, coupling)


def solution(mesh):
    in_specs = (
        P("child", "row", "col"),
        P("child", "row", "col"),
        P("row", "col"),
        P("col", "row"),
        P("child", None),
        P("row"),
    )
    out_specs = (P("row", ("child", "col")), P("row", None, ("child", "col"), None))
    return jax.shard_map(local, mesh=mesh, in_specs=in_specs, out_specs=out_specs, check_vma=False)
```

profile of v0, /device:TPU:0, one launch (start us, length us, event | category | flops | bytes accessed | tf_op | source)
XLA Modules:
  0.0 54.4 jit_solution(2019589471476399)
XLA Ops:
  1.3 51.6 %front_samples.1 = (f32[32,1024]{1,0:T(8,128)}, f32[1,2,32,256]{3,2,1,0:T(8,128)}) custom-call(s32[1]{0:T(128)S(6)} %copy.8.bound_ref, s32[4,4]{1,0:T(4,128)} %pattern_ref.1, f32[2,32,1024]{2,1,0:T(8,128)} %bitcast.4, f32[1,512,512]{2,1,0:T(8,128)} %contrib_ref.1, f32[1,512,1024]{2,1,0:T(8,128)} %assembled_ref.1, s32[1,2048]{1,0:T(1,128)} %maps_ref.1), custom_call_target="tpu_custom_call" | custom-call | tf_op jit(solution)/shard_map/front_samples/pallas_call | solution.py:478
  52.9 1.6 %deliver.1 = (f32[32,1024]{1,0:T(8,128)}, f32[1,2,32,256]{3,2,1,0:T(8,128)}) custom-call(f32[32,1024]{1,0:T(8,128)} %get-tuple-element.6.bases_ref, f32[1,2,32,256]{3,2,1,0:T(8,128)} %get-tuple-element.7.coupling_ref), custom_call_target="tpu_custom_call" | custom-call | tf_op jit(solution)/shard_map/deliver/pallas_call | solution.py:514
where the time goes:
time: 54.6 us; the launch traced here: 54.4 us
  Pallas kernels  53.2 us (97%)
  between operations  1.29 us (2%)
    pallas_call x1, Pallas kernels, local(): pl.pallas_call(whole_kernel, out_shape=(jax.ShapeDtypeStruct((width, wind...  51.6 us
    pallas_call x1, Pallas kernels, local(): pl.pallas_call(deliver_kernel, out_shape=(jax.ShapeDtypeStruct(bases.shap...  1.59 us

commit v1 on v0

v1 whole, which is shorter than its diff:
```python
import jax
import jax.numpy as jnp
from jax import lax
from jax.experimental import pallas as pl
from jax.experimental.pallas import tpu as pltpu
from jax.sharding import PartitionSpec as P

BT = 256
NB = 64
SUB = 8
CHUNK = 8
MESH = pl.DeviceIdType.MESH
VMEM = pl.BlockSpec(memory_space=pltpu.VMEM)
SMEM = pl.BlockSpec(memory_space=pltpu.SMEM)

NN = (((1,), (0,)), ((), ()))
NT = (((1,), (1,)), ((), ()))
TN = (((0,), (0,)), ((), ()))


def split(a):
    high = a.astype(jnp.bfloat16)
    low = (a - high.astype(jnp.float32)).astype(jnp.bfloat16)
    return high, low


def dot16(a, b, dims=NN):
    return lax.dot_general(a, b, dims, preferred_element_type=jnp.float32)


def mm3(a, b, dims=NN):
    (ah, al), (bh, bl) = split(a), split(b)
    return dot16(ah, bh, dims) + (dot16(ah, bl, dims) + dot16(al, bh, dims))


class Plane:
    def __init__(self):
        self.cols = lax.axis_size("col")
        self.chips = self.cols * lax.axis_size("child") // 2
        self.child = lax.axis_index("child")
        self.col = lax.axis_index("col")
        self.core = self.col % 2
        self.chip = (self.child * self.cols + self.col) // 2
        self.partner = {"col": self.col + 1 - 2 * self.core}
        self.across = [{"child": 1 - self.child}]
        step = 2
        while step < self.cols:
            self.across.append({"col": self.col + step - 2 * step * (self.col // step % 2)})
            step *= 2


def remote(source, target, send_sem, recv_sem, device):
    return pltpu.make_async_remote_copy(
        src_ref=source, dst_ref=target, send_sem=send_sem, recv_sem=recv_sem, device_id=device, device_id_type=MESH
    )


def greet(plane):
    count = lax.axis_size("row")
    me = lax.axis_index("row")
    barrier = pltpu.get_barrier_semaphore()

    @pl.when(me > 0)
    def _():
        pl.semaphore_signal(barrier, inc=1, device_id={"row": me - 1}, device_id_type=MESH)

    @pl.when(me < count - 1)
    def _():
        pl.semaphore_signal(barrier, inc=1, device_id={"row": me + 1}, device_id_type=MESH)

    near = [plane.partner] + plane.across
    for device in near:
        pl.semaphore_signal(barrier, inc=1, device_id=device, device_id_type=MESH)
    pl.semaphore_wait(barrier, len(near) + jnp.minimum(me, 1) + jnp.minimum(count - 1 - me, 1))


class Gather:
    def __init__(self, own_ref, out_ref, sems):
        self.own, self.out = own_ref, out_ref
        self.send_right, self.send_left, self.recv, self.swap_send, self.swap_recv, self.local_sem = sems
        self.count = lax.axis_size("row")
        self.me = lax.axis_index("row")
        self.half = lax.axis_index("child")
        self.chunks = own_ref.shape[1] // CHUNK
        self.has_left = self.me > 0
        self.has_right = self.me < self.count - 1

    def rows(self, chunk):
        return slice(chunk * CHUNK, (chunk + 1) * CHUNK)

    def hop(self, block, target, step, send, chunk):
        place = self.out.at[block, self.half, self.rows(chunk)]
        source = self.own.at[self.half, self.rows(chunk)] if step == 0 else place
        return remote(source, place, send.at[block, chunk], self.recv.at[block, chunk], {"row": target})

    def swap(self, block, chunk, half):
        place = self.out.at[block, half, self.rows(chunk)]
        sems = (self.swap_send.at[block, chunk], self.swap_recv.at[block, chunk])
        return remote(place, place, *sems, {"child": 1 - self.half})

    def pass_on(self, step, chunk):
        low, high = self.me - step, self.me + step
        if step > 0:

            @pl.when(low >= 0)
            def _():
                self.hop(low, self.me - 1, step, self.send_right, chunk).wait_recv()

        @pl.when(jnp.logical_and(low >= 0, self.has_right))
        def _():
            self.hop(low, self.me + 1, step, self.send_right, chunk).start()

        if step > 0:

            @pl.when(low >= 0)
            def _():
                self.swap(low, chunk, self.half).start()

            @pl.when(high < self.count)
            def _():
                self.hop(high, self.me + 1, step, self.send_left, chunk).wait_recv()

        @pl.when(jnp.logical_and(high < self.count, self.has_left))
        def _():
            self.hop(high, self.me - 1, step, self.send_left, chunk).start()

        if step > 0:

            @pl.when(high < self.count)
            def _():
                self.swap(high, chunk, self.half).start()

    def run(self, work):
        keep = pltpu.make_async_copy(self.own, self.out.at[self.me], self.local_sem)
        keep.start()
        for step in range(self.count):
            for chunk in range(self.chunks):
                self.pass_on(step, chunk)
                if step == 0 and chunk == self.chunks - 1:
                    keep.wait()
                for act in work.get((step, chunk), ()):
                    act()

    def nth(self, n):
        left, right = self.me, self.count - 1 - self.me
        both = jnp.minimum(left, right)
        near = (n + 1) // 2
        beside = self.me - near if n % 2 == 1 else self.me + near
        beyond = jnp.where(left < right, self.me + n - both, self.me - n + both)
        return jnp.where(n <= 2 * both, beside, beyond)

    def arrive(self, block):
        for chunk in range(self.chunks):
            self.swap(block, chunk, 1 - self.half).wait_recv()

    def drain(self):
        for step in range(self.count):
            low, high = self.me - step, self.me + step
            for chunk in range(self.chunks):

                @pl.when(jnp.logical_and(low >= 0, self.has_right))
                def _():
                    self.hop(low, self.me + 1, step, self.send_right, chunk).wait_send()

                @pl.when(jnp.logical_and(high < self.count, self.has_left))
                def _():
                    self.hop(high, self.me - 1, step, self.send_left, chunk).wait_send()

        for step in range(1, self.count):
            for chunk in range(self.chunks):
                self.swap(lax.rem(self.me + step, self.count), chunk, self.half).wait_send()


def prepare_sketch(pattern_ref, contrib, assembled, maps_ref, held):
    pick, place, front, entries = held
    half = lax.axis_index("child")
    tile_rows, tile_cols = contrib.shape
    window_rows = assembled.shape[1]
    row_pos, col_pos = lax.axis_index("row"), lax.axis_index("col")
    columns = maps_ref[:, pl.ds(pl.multiple_of(col_pos * tile_cols, tile_cols), tile_cols)] - col_pos * window_rows
    targets = maps_ref[:, pl.ds(pl.multiple_of(row_pos * tile_rows, tile_rows), tile_rows)] - row_pos * window_rows
    index = lax.broadcasted_iota(jnp.int32, (window_rows, tile_cols), 0)
    pick[...] = jnp.where(index == columns, 1.0, 0.0).astype(jnp.bfloat16)
    index = lax.broadcasted_iota(jnp.int32, (window_rows, tile_rows), 0)
    place[...] = jnp.where(index == targets, 1.0, 0.0).astype(jnp.bfloat16)
    front[0], front[1] = split(contrib[...])
    for row in range(tile_rows // BT):
        for col in range(window_rows // BT):
            where = (slice(row * BT, (row + 1) * BT), slice(col * BT, (col + 1) * BT))
            present = pattern_ref[half * (tile_rows // BT) + row, col].astype(jnp.float32)
            entries[(0,) + where], entries[(1,) + where] = split(assembled[where] * present)


def stacked(a, b, dims=NN):
    rows = a.shape[0] // 2
    both = dot16(a, b[0], dims)
    return both[:rows] + (dot16(a[:rows], b[1], dims) + both[rows:])


def sketch(omega, held, part_ref):
    pick, place, front, entries = held
    half = lax.axis_index("child")
    rows, tile_rows = omega.shape[0], place.shape[1]
    both = jnp.concatenate(split(omega), axis=0)
    picked = dot16(both, pick[...]).astype(jnp.bfloat16)
    product = stacked(picked, front, NT)
    sparse = stacked(both, entries, NT)
    spread = dot16(jnp.concatenate(split(product), axis=0), place[...], NT)
    part_ref[...] = spread[:rows] + spread[rows:]
    where = pl.ds(pl.multiple_of(half * tile_rows, tile_rows), tile_rows)
    part_ref[:, where] = part_ref[:, where] + sparse


class Total:
    def __init__(self, plane, part, sums, pair_buf, landed, window, offsets, sems):
        self.plane, self.part, self.sums, self.pair_buf = plane, part, sums, pair_buf
        self.landed, self.window = landed, window
        self.own, self.other = offsets
        self.pair_send, self.pair_recv, self.send, self.recv = sems
        self.phases = len(plane.across)

    def lanes(self, offset):
        return pl.ds(pl.multiple_of(offset, 128), self.window.shape[2])

    def pair(self, r):
        source = self.part.at[r, :, self.lanes(self.other)]
        return remote(source, self.pair_buf.at[r], self.pair_send.at[r], self.pair_recv.at[r], self.plane.partner)

    def cross(self, r, phase, side):
        half = self.window.shape[1] // 2
        rows = slice(side * half, (side + 1) * half)
        device = self.plane.across[(phase + side) % self.phases]
        sems = (self.send.at[r, phase, side], self.recv.at[r, phase, side])
        return remote(self.sums.at[r, phase, rows], self.landed.at[r, phase, rows], *sems, device), rows

    def begin(self, r):
        self.pair(r).start()

    def advance(self, r, phase):
        if phase == 0:
            self.pair(r).wait_recv()
            self.sums[r, 0] = self.part[r, :, self.lanes(self.own)] + self.pair_buf[r]
            for side in range(2):
                self.cross(r, 0, side)[0].start()
            return
        for side in range(2):
            copy, rows = self.cross(r, phase - 1, side)
            copy.wait_recv()
            total = self.sums[r, phase - 1, rows] + self.landed[r, phase - 1, rows]
            if phase < self.phases:
                self.sums[r, phase, rows] = total
                self.cross(r, phase, side)[0].start()
            else:
                self.window[r, rows] = total

    def drain(self, stages):
        for r in range(stages):
            self.pair(r).wait_send()
            for phase in range(self.phases):
                for side in range(2):
                    self.cross(r, phase, side)[0].wait_send()


def eliminate(leaves):
    groups = NB // SUB
    index = lax.broadcasted_iota(jnp.int32, (SUB, 2 * NB), 0)
    wide = (SUB, 2 * NB)
    leaves = [list(rows) for rows in leaves]
    for panel in range(groups):
        first = panel * SUB
        columns = [
            {
                q: [jnp.broadcast_to(rows[q][:, first + k : first + k + 1], wide) for k in range(SUB)]
                for q in range(panel, groups)
            }
            for rows in leaves
        ]
        for k in range(SUB):
            for rows, cols in zip(leaves, columns):
                own = cols[panel]
                scale = lax.rsqrt(jnp.broadcast_to(own[k][k : k + 1], wide))
                pivot = jnp.broadcast_to(rows[panel][k : k + 1], wide) * scale
                weight = {q: cols[q][k] * scale for q in range(panel, groups)}
                across = weight[panel]
                below = jnp.where(index > k, across, 0.0)
                rows[panel] = jnp.where(index == k, pivot, rows[panel] - below * pivot)
                for j in range(k + 1, SUB):
                    factor = jnp.broadcast_to(across[j : j + 1], wide)
                    for q in range(panel, groups):
                        cols[q][j] = cols[q][j] - (below if q == panel else weight[q]) * factor
                for q in range(panel + 1, groups):
                    rows[q] = rows[q] - weight[q] * pivot
    return leaves


def factor(gram, work, done_block):
    columns = gram.shape[0]
    eye = jnp.where(
        lax.broadcasted_iota(jnp.int32, (columns, columns), 0)
        == lax.broadcasted_iota(jnp.int32, (columns, columns), 1),
        1.0,
        0.0,
    )
    work[:, :columns] = gram
    work[:, columns:] = eye
    small_eye = eye[:NB, :NB]
    for block in range(columns // NB):
        begin, end = block * NB, (block + 1) * NB
        diagonal = jnp.concatenate([work[begin:end, begin:end], small_eye], axis=1)
        done = eliminate([[diagonal[q * SUB : (q + 1) * SUB] for q in range(NB // SUB)]])
        inverse = jnp.concatenate(done[0], axis=0)[:, NB:]
        rows = mm3(inverse, work[begin:end, :])
        work[begin:end, :] = rows
        done_block(block, begin, end, rows[:, :columns])
        if end < columns:
            work[end:, :] = work[end:, :] - mm3(rows[:, end:columns], rows, TN)


def whole_kernel(
    bound_ref, pattern_ref, omega_ref, contrib_ref, assembled_ref, maps_ref, bases_ref, coupling_ref,
    gathered, contrib_buf, assembled_buf, pick, place, front, entries,
    part, sums, pair_buf, landed, window, work, upper, sibling, bases_out, bases_in, coupling_out, coupling_in,
    input_sems, *sems,
):
    plane = Plane()
    core = plane.core
    window_rows = assembled_buf.shape[1]
    columns, width = upper.shape[1], bases_ref.shape[0]
    stages, span = window.shape[0], window.shape[2]
    low = window_rows - span
    held = (pick, place, front, entries)
    load_front = pltpu.make_async_copy(contrib_ref.at[0], contrib_buf, input_sems.at[0])
    load_entries = pltpu.make_async_copy(assembled_ref.at[0], assembled_buf, input_sems.at[1])
    load_front.start()
    load_entries.start()
    greet(plane)

    row_count, row_pos = lax.axis_size("row"), lax.axis_index("row")
    gather = Gather(omega_ref, gathered, sems[:6])
    summing = Total(plane, part, sums, pair_buf, landed, window, (core * low, (1 - core) * low), sems[6:10])
    last = len(plane.across)

    def prepare():
        load_front.wait()
        load_entries.wait()
        prepare_sketch(pattern_ref, contrib_buf, assembled_buf, maps_ref, held)

    def stage(n):
        block = row_pos if n == 0 else gather.nth(n)
        if n > 0:
            gather.arrive(block)
        sketch(gathered[block].reshape(columns // stages, window_rows), held, part.at[block])
        summing.begin(block)

    def advance(n, phase):
        summing.advance(row_pos if n == 0 else gather.nth(n), phase)

    if stages == row_count:
        chunks = gather.chunks
        waiting = [(n, phase) for n in range(stages - 2) for phase in range(last + 1)]
        work_at = {(0, chunks - 1): [prepare, lambda: stage(0)]}
        taken = []

        def put(step, chunk, act, key):
            work_at.setdefault((min(step, row_count - 1), min(chunk, chunks - 1)), []).append(act)
            taken.append(key)

        put(1, chunks // 2, lambda: advance(0, 0), (0, 0))
        put(2, chunks - 1, lambda: advance(0, 1), (0, 1))
        first = None
        if stages > 2:
            put(3, 0, lambda: stage(1), "stage 1")
            put(3, chunks // 2, lambda: advance(1, 0), (1, 0))
        gather.run(work_at)
        pending = {n: [p for p in range(last + 1) if (n, p) not in taken] for n in range(stages)}
        started = [0] + ([1] if stages > 2 else [])

        def go():
            for n in started:
                if pending[n]:
                    phase = pending[n].pop(0)
                    advance(n, phase)

        for n in range(stages):
            if n in started:
                continue
            stage(n)
            started.append(n)
            go()
        while any(pending.values()):
            go()
    else:
        gather.run({(0, 0): [prepare]})
        for step in range(1, row_count):
            gather.arrive(lax.rem(row_pos + step, row_count))
        sketch(gathered[...].reshape(columns, window_rows), held, part.at[0])
        summing.begin(0)
        for phase in range(last + 1):
            summing.advance(0, phase)

    near_send, near_recv, end_send, end_recv = sems[10:]
    near = {"row": row_pos + 1 - 2 * (row_pos % 2)}

    def send(block):
        start = block * NB // 128 * 128
        rows = slice(block * NB, (block + 1) * NB)
        source, target = upper.at[rows, start:], sibling.at[rows, start:]
        return remote(source, target, near_send.at[block], near_recv.at[block], near)

    def done_block(block, begin, end, rows):
        keep = lax.broadcasted_iota(jnp.int32, rows.shape, 1) >= begin + lax.broadcasted_iota(
            jnp.int32, rows.shape, 0
        )
        upper[begin:end, :] = jnp.where(keep, rows, 0.0)
        send(block).start()

    bound = bound_ref[0]
    samples = window[...].reshape(columns, span)
    place_of = lax.broadcasted_iota(jnp.int32, (columns, span), 1) + core * low
    masked = jnp.where((1 - 2 * core) * (bound - place_of) + core > 0, samples, 0.0)
    rows_of_leaf = (1 - core) * bound + core * (window_rows - bound)
    factor(mm3(masked, masked, NT) / rows_of_leaf.astype(jnp.float32), work, done_block)

    pair_rows = pl.ds(pl.multiple_of(plane.chip * 2 * width, 2 * width), 2 * width)
    give_bases = remote(
        bases_out.at[1 - core], bases_in.at[core], end_send.at[0], end_recv.at[0], plane.partner
    )
    give_coupling = remote(
        coupling_out.at[1 - core], coupling_in.at[core], end_send.at[1], end_recv.at[1], plane.partner
    )
    bases_out[...] = mm3(work[pair_rows, columns:], samples).reshape(bases_out.shape)
    give_bases.start()
    own = upper[pair_rows, :]
    for block in range(columns // NB):
        start = block * NB // 128 * 128
        send(block).wait_recv()
        piece = mm3(own[:, start:], sibling[block * NB : (block + 1) * NB, start:], NT)
        coupling_out[:, :, block * NB : (block + 1) * NB] = piece.reshape(2, width, NB)
    give_coupling.start()
    bases_in[core] = bases_out[core]
    coupling_ref[0, core] = coupling_out[core]
    remote(
        bases_out.at[core], bases_in.at[1 - core], end_send.at[0], end_recv.at[0], plane.partner
    ).wait_recv()
    bases_ref[:, :low] = bases_in[0, :, :low]
    bases_ref[:, span:] = bases_in[1, :, span - low :]
    lane = lax.broadcasted_iota(jnp.int32, (width, span - low), 1) + low
    bases_ref[:, low:span] = jnp.where(lane < bound, bases_in[0, :, low:], bases_in[1, :, : span - low])
    remote(
        coupling_out.at[core], coupling_in.at[1 - core], end_send.at[1], end_recv.at[1], plane.partner
    ).wait_recv()
    coupling_ref[0, 1 - core] = coupling_in[1 - core]

    gather.drain()
    summing.drain(stages)
    for block in range(columns // NB):
        send(block).wait_send()
    give_bases.wait_send()
    give_coupling.wait_send()


def deliver_kernel(bases_ref, coupling_ref, bases_out, coupling_out):
    bases_out[...] = bases_ref[...]
    coupling_out[...] = coupling_ref[...]


def local(contrib, assembled, pattern, omega, row_maps, leaf_bounds):
    tile_rows, tile_cols = contrib.shape[1:]
    window_rows, own_width = omega.shape
    rows = lax.axis_size("row")
    cols = lax.axis_size("col")
    chips = cols * lax.axis_size("child") // 2
    columns = own_width * rows
    width = columns // (2 * chips)
    phases = 1 + (cols // 2).bit_length() - 1
    span = (window_rows // 2 + window_rows // 16 + 127) // 128 * 128
    own = omega.T.reshape(2, own_width // 2, window_rows)
    f32, bf16, dma = jnp.float32, jnp.bfloat16, pltpu.SemaphoreType.DMA
    any_space = pl.BlockSpec(memory_space=pl.ANY)
    stages = rows if own_width >= 8 * SUB else 1
    depth = columns // stages
    chunks = own_width // 2 // CHUNK
    bases, coupling = pl.pallas_call(
        whole_kernel,
        out_shape=(
            jax.ShapeDtypeStruct((width, window_rows), f32),
            jax.ShapeDtypeStruct((1, 2, width, columns), f32),
        ),
        in_specs=[SMEM, SMEM, VMEM, any_space, any_space, VMEM],
        out_specs=(VMEM, VMEM),
        scratch_shapes=[
            pltpu.VMEM((rows, 2, own_width // 2, window_rows), f32),
            pltpu.VMEM((tile_rows, tile_cols), f32),
            pltpu.VMEM((tile_rows, window_rows), f32),
            pltpu.VMEM((window_rows, tile_cols), bf16),
            pltpu.VMEM((window_rows, tile_rows), bf16),
            pltpu.VMEM((2, tile_rows, tile_cols), bf16),
            pltpu.VMEM((2, tile_rows, window_rows), bf16),
            pltpu.VMEM((stages, depth, window_rows), f32),
            pltpu.VMEM((stages, phases, depth, span), f32),
            pltpu.VMEM((stages, depth, span), f32),
            pltpu.VMEM((stages, phases, depth, span), f32),
            pltpu.VMEM((stages, depth, span), f32),
            pltpu.VMEM((columns, 2 * columns), f32),
            pltpu.VMEM((columns, columns), f32),
            pltpu.VMEM((columns, columns), f32),
            pltpu.VMEM((2, width, span), f32),
            pltpu.VMEM((2, width, span), f32),
            pltpu.VMEM((2, width, columns), f32),
            pltpu.VMEM((2, width, columns), f32),
            dma((2,)),
        ]
        + [dma((rows, chunks))] * 5
        + [dma]
        + [dma((stages,))] * 2
        + [dma((stages, phases, 2))] * 2
        + [dma((columns // NB,))] * 2
        + [dma((2,))] * 2,
        compiler_params=pltpu.CompilerParams(
            collective_id=0, has_side_effects=True, vmem_limit_bytes=56 << 20
        ),
        name="front_samples",
    )(leaf_bounds, pattern, own, contrib, assembled, row_maps)
    bases, coupling = pl.pallas_call(
        deliver_kernel,
        out_shape=(
            jax.ShapeDtypeStruct(bases.shape, f32),
            jax.ShapeDtypeStruct(coupling.shape, f32),
        ),
        in_specs=[VMEM, VMEM],
        out_specs=(VMEM, VMEM),
        name="deliver",
    )(bases, coupling)
    return (bases.T, coupling)


def solution(mesh):
    in_specs = (
        P("child", "row", "col"),
        P("child", "row", "col"),
        P("row", "col"),
        P("col", "row"),
        P("child", None),
        P("row"),
    )
    out_specs = (P("row", ("child", "col")), P("row", None, ("child", "col"), None))
    return jax.shard_map(local, mesh=mesh, in_specs=in_specs, out_specs=out_specs, check_vma=False)
```

time: 54.6 us -> 56.2 us (1.029)
  Pallas kernels: 53.2 us -> 54.8 us
    pallas_call x1, Pallas kernels: 51.6 us -> 53.2 us  [local(): pl.pallas_call(whole_kernel, out_shape=(jax.ShapeDtypeStruct((width, wind...]
where the time goes in v1:
time: 56.2 us; the launch traced here: 56.1 us
  Pallas kernels  54.8 us (98%)
  between operations  1.29 us (2%)
    pallas_call x1, Pallas kernels, local(): pl.pallas_call(whole_kernel, out_shape=(jax.ShapeDtypeStruct((width, wind...  53.2 us
    pallas_call x1, Pallas kernels, local(): pl.pallas_call(deliver_kernel, out_shape=(jax.ShapeDtypeStruct(bases.shap...  1.59 us

profile of v1, /device:TPU:0, one launch (start us, length us, event | category | flops | bytes accessed | tf_op | source)
XLA Modules:
  0.0 56.1 jit_solution(6683840302082083822)
XLA Ops:
  1.3 53.2 %front_samples.1 = (f32[32,1024]{1,0:T(8,128)}, f32[1,2,32,256]{3,2,1,0:T(8,128)}) custom-call(s32[1]{0:T(128)S(6)} %copy.8.bound_ref, s32[4,4]{1,0:T(4,128)} %pattern_ref.1, f32[2,32,1024]{2,1,0:T(8,128)} %bitcast.4, f32[1,512,512]{2,1,0:T(8,128)} %contrib_ref.1, f32[1,512,1024]{2,1,0:T(8,128)} %assembled_ref.1, s32[1,2048]{1,0:T(1,128)} %maps_ref.1), custom_call_target="tpu_custom_call" | custom-call | tf_op jit(solution)/shard_map/front_samples/pallas_call | solution.py:483
  54.5 1.6 %deliver.1 = (f32[32,1024]{1,0:T(8,128)}, f32[1,2,32,256]{3,2,1,0:T(8,128)}) custom-call(f32[32,1024]{1,0:T(8,128)} %get-tuple-element.6.bases_ref, f32[1,2,32,256]{3,2,1,0:T(8,128)} %get-tuple-element.7.coupling_ref), custom_call_target="tpu_custom_call" | custom-call | tf_op jit(solution)/shard_map/deliver/pallas_call | solution.py:524

commit v2 on v1

--- a/solution.py
+++ b/solution.py
@@ -9,6 +9,9 @@
 NB = 64
 SUB = 8
 CHUNK = 8
+ROOM = 8 << 20
+SMALL = 62 << 20
+DOUBLED = 1
 MESH = pl.DeviceIdType.MESH
 VMEM = pl.BlockSpec(memory_space=pltpu.VMEM)
 SMEM = pl.BlockSpec(memory_space=pltpu.SMEM)
@@ -47,6 +50,7 @@
         while step < self.cols:
             self.across.append({"col": self.col + step - 2 * step * (self.col // step % 2)})
             step *= 2
+        self.high = self.col // 2 % 2
 
 
 def remote(source, target, send_sem, recv_sem, device):
@@ -212,53 +216,106 @@
 
 
 class Total:
-    def __init__(self, plane, part, sums, pair_buf, landed, window, offsets, sems):
+    def __init__(self, plane, part, sums, pair_buf, landed, window, sems):
         self.plane, self.part, self.sums, self.pair_buf = plane, part, sums, pair_buf
         self.landed, self.window = landed, window
-        self.own, self.other = offsets
-        self.pair_send, self.pair_recv, self.send, self.recv = sems
+        self.pair_send, self.pair_recv, self.send, self.recv, self.hand_send, self.hand_recv = sems
         self.phases = len(plane.across)
-
-    def lanes(self, offset):
-        return pl.ds(pl.multiple_of(offset, 128), self.window.shape[2])
+        self.depth, self.half = pair_buf.shape[1:]
+        self.shared = window.shape[2] - self.half
+        self.place = self.lanes(plane.core * self.shared, self.half)
+
+    def lanes(self, offset, size):
+        return pl.ds(pl.multiple_of(offset, 128), size)
+
+    def side(self, which):
+        return pl.ds(pl.multiple_of(which * (self.depth // 2), SUB), self.depth // 2)
 
     def pair(self, r):
-        source = self.part.at[r, :, self.lanes(self.other)]
+        source = self.part.at[r, :, self.lanes((1 - self.plane.core) * self.half, self.half)]
         return remote(source, self.pair_buf.at[r], self.pair_send.at[r], self.pair_recv.at[r], self.plane.partner)
 
+    def hand(self, r):
+        core, half, shared = self.plane.core, self.half, self.shared
+        source = self.window.at[r, :, self.lanes((1 - core) * (half - shared) + core * shared, shared)]
+        target = self.window.at[r, :, self.lanes(core * half, shared)]
+        return remote(source, target, self.hand_send.at[r], self.hand_recv.at[r], self.plane.partner)
+
     def cross(self, r, phase, side):
-        half = self.window.shape[1] // 2
-        rows = slice(side * half, (side + 1) * half)
         device = self.plane.across[(phase + side) % self.phases]
+        rows = self.side(side)
         sems = (self.send.at[r, phase, side], self.recv.at[r, phase, side])
-        return remote(self.sums.at[r, phase, rows], self.landed.at[r, phase, rows], *sems, device), rows
+        return remote(self.sums.at[r, phase, rows], self.landed.at[r, phase, rows], *sems, device)
+
+    def scatter(self, r, phase, arriving=False):
+        keep, away = self.plane.high, 1 - self.plane.high
+        sems = (self.send.at[r, phase, 0], self.recv.at[r, phase, 0])
+        if phase == 0:
+            rows = self.side(keep if arriving else away)
+            return remote(self.sums.at[r, 0, rows], self.landed.at[r, 0, rows], *sems, self.plane.across[1])
+        if phase == 1:
+            rows = self.side(keep)
+            return remote(self.sums.at[r, 1, rows], self.landed.at[r, 1, rows], *sems, self.plane.across[0])
+        place = self.window.at[r, self.side(away if arriving else keep), self.place]
+        return remote(place, place, *sems, self.plane.across[1])
 
     def begin(self, r):
         self.pair(r).start()
 
-    def advance(self, r, phase):
+    def steps(self, double):
+        return self.phases + 1 if double else 4
+
+    def advance(self, r, phase, double):
         if phase == 0:
             self.pair(r).wait_recv()
-            self.sums[r, 0] = self.part[r, :, self.lanes(self.own)] + self.pair_buf[r]
+            own = self.lanes(self.plane.core * self.half, self.half)
+            self.sums[r, 0] = self.part[r, :, own] + self.pair_buf[r]
+            if double:
+                for side in range(2):
+                    self.cross(r, 0, side).start()
+            else:
+                self.scatter(r, 0).start()
+            return
+        if double:
             for side in range(2):
-                self.cross(r, 0, side)[0].start()
+                rows = self.side(side)
+                self.cross(r, phase - 1, side).wait_recv()
+                total = self.sums[r, phase - 1, rows] + self.landed[r, phase - 1, rows]
+                if phase < self.phases:
+                    self.sums[r, phase, rows] = total
+                    self.cross(r, phase, side).start()
+                else:
+                    self.window[r, rows, self.place] = total
+            if phase == self.phases:
+                self.hand(r).start()
             return
-        for side in range(2):
-            copy, rows = self.cross(r, phase - 1, side)
-            copy.wait_recv()
-            total = self.sums[r, phase - 1, rows] + self.landed[r, phase - 1, rows]
-            if phase < self.phases:
-                self.sums[r, phase, rows] = total
-                self.cross(r, phase, side)[0].start()
-            else:
-                self.window[r, rows] = total
-
-    def drain(self, stages):
-        for r in range(stages):
-            self.pair(r).wait_send()
+        self.scatter(r, phase - 1, True).wait_recv()
+        if phase == 3:
+            self.hand(r).start()
+            return
+        rows = self.side(self.plane.high)
+        total = self.sums[r, phase - 1, rows] + self.landed[r, phase - 1, rows]
+        if phase == 1:
+            self.sums[r, 1, rows] = total
+        else:
+            self.window[r, rows, self.place] = total
+        self.scatter(r, phase).start()
+
+    def arrive(self, r):
+        core, half, shared = self.plane.core, self.half, self.shared
+        target = self.window.at[r, :, self.lanes((1 - core) * half, shared)]
+        remote(target, target, self.hand_send.at[r], self.hand_recv.at[r], self.plane.partner).wait_recv()
+
+    def drain(self, r, double):
+        self.pair(r).wait_send()
+        self.hand(r).wait_send()
+        if double:
             for phase in range(self.phases):
                 for side in range(2):
-                    self.cross(r, phase, side)[0].wait_send()
+                    self.cross(r, phase, side).wait_send()
+        else:
+            for phase in range(3):
+                self.scatter(r, phase).wait_send()
 
 
 def eliminate(leaves):
@@ -317,8 +374,8 @@
 
 
 def whole_kernel(
-    bound_ref, pattern_ref, omega_ref, contrib_ref, assembled_ref, maps_ref, bases_ref, coupling_ref,
-    gathered, contrib_buf, assembled_buf, pick, place, front, entries,
+    bound_ref, pattern_hbm, omega_ref, contrib_ref, assembled_ref, maps_hbm, bases_ref, coupling_ref,
+    pattern_ref, maps_ref, gathered, contrib_buf, assembled_buf, pick, place, front, entries,
     part, sums, pair_buf, landed, window, work, upper, sibling, bases_out, bases_in, coupling_out, coupling_in,
     input_sems, *sems,
 ):
@@ -331,74 +388,82 @@
     held = (pick, place, front, entries)
     load_front = pltpu.make_async_copy(contrib_ref.at[0], contrib_buf, input_sems.at[0])
     load_entries = pltpu.make_async_copy(assembled_ref.at[0], assembled_buf, input_sems.at[1])
-    load_front.start()
-    load_entries.start()
+    load_small = [
+        pltpu.make_async_copy(source, target, input_sems.at[2 + i])
+        for i, (source, target) in enumerate(
+            ((maps_hbm, maps_ref), (pattern_hbm, pattern_ref))
+        )
+    ]
+    for copy in load_small + [load_front, load_entries]:
+        copy.start()
     greet(plane)
 
     row_count, row_pos = lax.axis_size("row"), lax.axis_index("row")
     gather = Gather(omega_ref, gathered, sems[:6])
-    summing = Total(plane, part, sums, pair_buf, landed, window, (core * low, (1 - core) * low), sems[6:10])
-    last = len(plane.across)
+    summing = Total(plane, part, sums, pair_buf, landed, window, sems[6:12])
 
     def prepare():
-        load_front.wait()
-        load_entries.wait()
+        for copy in load_small + [load_front, load_entries]:
+            copy.wait()
         prepare_sketch(pattern_ref, contrib_buf, assembled_buf, maps_ref, held)
 
+    def block_of(n):
+        return row_pos if n == 0 else gather.nth(n)
+
+    def double(n):
+        return n >= stages - DOUBLED
+
     def stage(n):
-        block = row_pos if n == 0 else gather.nth(n)
+        block = block_of(n)
         if n > 0:
             gather.arrive(block)
         sketch(gathered[block].reshape(columns // stages, window_rows), held, part.at[block])
         summing.begin(block)
 
-    def advance(n, phase):
-        summing.advance(row_pos if n == 0 else gather.nth(n), phase)
-
     if stages == row_count:
-        chunks = gather.chunks
-        waiting = [(n, phase) for n in range(stages - 2) for phase in range(last + 1)]
-        work_at = {(0, chunks - 1): [prepare, lambda: stage(0)]}
-        taken = []
-
-        def put(step, chunk, act, key):
-            work_at.setdefault((min(step, row_count - 1), min(chunk, chunks - 1)), []).append(act)
-            taken.append(key)
-
-        put(1, chunks // 2, lambda: advance(0, 0), (0, 0))
-        put(2, chunks - 1, lambda: advance(0, 1), (0, 1))
-        first = None
-        if stages > 2:
-            put(3, 0, lambda: stage(1), "stage 1")
-            put(3, chunks // 2, lambda: advance(1, 0), (1, 0))
-        gather.run(work_at)
-        pending = {n: [p for p in range(last + 1) if (n, p) not in taken] for n in range(stages)}
-        started = [0] + ([1] if stages > 2 else [])
-
-        def go():
-            for n in started:
-                if pending[n]:
-                    phase = pending[n].pop(0)
-                    advance(n, phase)
-
-        for n in range(stages):
-            if n in started:
-                continue
+        begun, left = [], {}
+
+        def begin(n):
             stage(n)
-            started.append(n)
-            go()
-        while any(pending.values()):
-            go()
+            begun.append(n)
+            left[n] = list(range(summing.steps(double(n))))
+
+        def go(n):
+            if n in left and left[n]:
+                summing.advance(block_of(n), left[n].pop(0), double(n))
+
+        def go_all():
+            for n in list(begun):
+                go(n)
+
+        end, mid = gather.chunks - 1, gather.chunks // 2
+        queue = {(0, end): [prepare, lambda: begin(0)]}
+        queue.setdefault((1, mid), []).append(lambda: go(0))
+        queue.setdefault((2, end), []).append(lambda: go(0))
+        if row_count > 3:
+            queue.setdefault((3, 0), []).append(lambda: begin(1))
+        gather.run(queue)
+        go(1)
+        for n in range(len(begun), stages):
+            begin(n)
+            go_all()
+        while any(left.values()):
+            go_all()
+        blocks = range(stages)
+        for n in blocks:
+            summing.arrive(block_of(n))
     else:
         gather.run({(0, 0): [prepare]})
         for step in range(1, row_count):
             gather.arrive(lax.rem(row_pos + step, row_count))
         sketch(gathered[...].reshape(columns, window_rows), held, part.at[0])
         summing.begin(0)
-        for phase in range(last + 1):
-            summing.advance(0, phase)
-
-    near_send, near_recv, end_send, end_recv = sems[10:]
+        for phase in range(summing.steps(True)):
+            summing.advance(0, phase, True)
+        summing.arrive(0)
+        blocks = []
+
+    near_send, near_recv, end_send, end_recv = sems[12:]
     near = {"row": row_pos + 1 - 2 * (row_pos % 2)}
 
     def send(block):
@@ -414,7 +479,7 @@
         upper[begin:end, :] = jnp.where(keep, rows, 0.0)
         send(block).start()
 
-    bound = bound_ref[0]
+    bound = bound_ref[...]
     samples = window[...].reshape(columns, span)
     place_of = lax.broadcasted_iota(jnp.int32, (columns, span), 1) + core * low
     masked = jnp.where((1 - 2 * core) * (bound - place_of) + core > 0, samples, 0.0)
@@ -452,7 +517,10 @@
     coupling_ref[0, 1 - core] = coupling_in[1 - core]
 
     gather.drain()
-    summing.drain(stages)
+    for n in blocks:
+        summing.drain(block_of(n), double(n))
+    if not blocks:
+        summing.drain(0, True)
     for block in range(columns // NB):
         send(block).wait_send()
     give_bases.wait_send()
@@ -486,9 +554,11 @@
             jax.ShapeDtypeStruct((width, window_rows), f32),
             jax.ShapeDtypeStruct((1, 2, width, columns), f32),
         ),
-        in_specs=[SMEM, SMEM, VMEM, any_space, any_space, VMEM],
+        in_specs=[VMEM] + [any_space] * 5,
         out_specs=(VMEM, VMEM),
         scratch_shapes=[
+            pltpu.SMEM(pattern.shape, jnp.int32),
+            pltpu.VMEM(row_maps.shape, jnp.int32),
             pltpu.VMEM((rows, 2, own_width // 2, window_rows), f32),
             pltpu.VMEM((tile_rows, tile_cols), f32),
             pltpu.VMEM((tile_rows, window_rows), f32),
@@ -497,9 +567,9 @@
             pltpu.VMEM((2, tile_rows, tile_cols), bf16),
             pltpu.VMEM((2, tile_rows, window_rows), bf16),
             pltpu.VMEM((stages, depth, window_rows), f32),
-            pltpu.VMEM((stages, phases, depth, span), f32),
-            pltpu.VMEM((stages, depth, span), f32),
-            pltpu.VMEM((stages, phases, depth, span), f32),
+            pltpu.VMEM((stages, phases, depth, window_rows // 2), f32),
+            pltpu.VMEM((stages, depth, window_rows // 2), f32),
+            pltpu.VMEM((stages, phases, depth, window_rows // 2), f32),
             pltpu.VMEM((stages, depth, span), f32),
             pltpu.VMEM((columns, 2 * columns), f32),
             pltpu.VMEM((columns, columns), f32),
@@ -508,19 +578,20 @@
             pltpu.VMEM((2, width, span), f32),
             pltpu.VMEM((2, width, columns), f32),
             pltpu.VMEM((2, width, columns), f32),
-            dma((2,)),
+            dma((4,)),
         ]
         + [dma((rows, chunks))] * 5
         + [dma]
         + [dma((stages,))] * 2
-        + [dma((stages, phases, 2))] * 2
+        + [dma((stages, max(phases, 3), 2))] * 2
+        + [dma((stages,))] * 2
         + [dma((columns // NB,))] * 2
         + [dma((2,))] * 2,
         compiler_params=pltpu.CompilerParams(
-            collective_id=0, has_side_effects=True, vmem_limit_bytes=56 << 20
+            collective_id=0, has_side_effects=True, vmem_limit_bytes=(64 << 20) - ROOM
         ),
         name="front_samples",
-    )(leaf_bounds, pattern, own, contrib, assembled, row_maps)
+    )(leaf_bounds.reshape(1, 1), pattern, own, contrib, assembled, row_maps)
     bases, coupling = pl.pallas_call(
         deliver_kernel,
         out_shape=(
@@ -529,6 +600,7 @@
         ),
         in_specs=[VMEM, VMEM],
         out_specs=(VMEM, VMEM),
+        compiler_params=pltpu.CompilerParams(vmem_limit_bytes=SMALL),
         name="deliver",
     )(bases, coupling)
     return (bases.T, coupling)

time: 56.2 us -> 51.2 us (0.911)
  Pallas kernels: 54.8 us -> 49.8 us
    pallas_call x1, Pallas kernels: 53.2 us -> 48.2 us  [local(): pl.pallas_call(whole_kernel, out_shape=(jax.ShapeDtypeStruct((width, wind...]
where the time goes in v2:
time: 51.2 us; the launch traced here: 51.1 us
  Pallas kernels  49.8 us (97%)
  between operations  1.29 us (3%)
    pallas_call x1, Pallas kernels, local(): pl.pallas_call(whole_kernel, out_shape=(jax.ShapeDtypeStruct((width, wind...  48.2 us
    pallas_call x1, Pallas kernels, local(): pl.pallas_call(deliver_kernel, out_shape=(jax.ShapeDtypeStruct(bases.shap...  1.59 us

profile of v2, /device:TPU:0, one launch (start us, length us, event | category | flops | bytes accessed | tf_op | source)
XLA Modules:
  0.0 51.1 jit_solution(317974379625770488)
XLA Ops:
  1.3 48.2 %front_samples.1 = (f32[32,1024]{1,0:T(8,128)}, f32[1,2,32,256]{3,2,1,0:T(8,128)}) custom-call(s32[1,1]{1,0:T(1,128)} %bitcast.5.bound_ref, s32[4,4]{1,0:T(4,128)} %pattern_hbm.1, f32[2,32,1024]{2,1,0:T(8,128)} %bitcast.6, f32[1,512,512]{2,1,0:T(8,128)} %contrib_ref.1, f32[1,512,1024]{2,1,0:T(8,128)} %assembled_ref.1, s32[1,2048]{1,0:T(1,128)} %maps_hbm.1), custom_call_target="tpu_custom_call" | custom-call | tf_op jit(solution)/shard_map/front_samples/pallas_call | solution.py:551
  49.5 1.6 %deliver.1 = (f32[32,1024]{1,0:T(8,128)}, f32[1,2,32,256]{3,2,1,0:T(8,128)}) custom-call(f32[32,1024]{1,0:T(8,128)} %get-tuple-element.6.bases_ref, f32[1,2,32,256]{3,2,1,0:T(8,128)} %get-tuple-element.7.coupling_ref), custom_call_target="tpu_custom_call" | custom-call | tf_op jit(solution)/shard_map/deliver/pallas_call | solution.py:595

commit v3 on v2

--- a/solution.py
+++ b/solution.py
@@ -6,9 +6,11 @@
 from jax.sharding import PartitionSpec as P
 
 BT = 256
-NB = 64
+NB = 128
+PIECE = 64
 SUB = 8
 CHUNK = 8
+TWINS = 1
 ROOM = 8 << 20
 SMALL = 62 << 20
 DOUBLED = 1
@@ -81,11 +83,13 @@
 class Gather:
     def __init__(self, own_ref, out_ref, sems):
         self.own, self.out = own_ref, out_ref
-        self.send_right, self.send_left, self.recv, self.swap_send, self.swap_recv, self.local_sem = sems
+        self.send_right, self.send_left, self.recv, self.swap_send, self.swap_recv = sems[:5]
+        self.twin_send, self.twin_recv, self.local_sem = sems[5:]
         self.count = lax.axis_size("row")
         self.me = lax.axis_index("row")
         self.half = lax.axis_index("child")
         self.chunks = own_ref.shape[1] // CHUNK
+        self.first_twin = self.chunks - min(TWINS, self.chunks - 1)
         self.has_left = self.me > 0
         self.has_right = self.me < self.count - 1
 
@@ -102,37 +106,46 @@
         sems = (self.swap_send.at[block, chunk], self.swap_recv.at[block, chunk])
         return remote(place, place, *sems, {"child": 1 - self.half})
 
+    def twin(self, block, target, step, chunk):
+        place = self.out.at[block, 1 - self.half, self.rows(chunk)]
+        source = self.own.at[1 - self.half, self.rows(chunk)] if step == 0 else place
+        sems = (self.twin_send.at[block, chunk], self.twin_recv.at[block, chunk])
+        return remote(source, place, *sems, {"row": target})
+
     def pass_on(self, step, chunk):
         low, high = self.me - step, self.me + step
-        if step > 0:
-
-            @pl.when(low >= 0)
+        ways = (
+            (low, low >= 0, low == 0, self.has_right, 1, self.send_right),
+            (high, high < self.count, high == self.count - 1, self.has_left, -1, self.send_left),
+        )
+        for block, there, outer, onward, way, sems in ways:
+            if step > 0:
+
+                @pl.when(there)
+                def _():
+                    self.hop(block, self.me - way, step, sems, chunk).wait_recv()
+
+            @pl.when(jnp.logical_and(there, onward))
             def _():
-                self.hop(low, self.me - 1, step, self.send_right, chunk).wait_recv()
-
-        @pl.when(jnp.logical_and(low >= 0, self.has_right))
-        def _():
-            self.hop(low, self.me + 1, step, self.send_right, chunk).start()
-
-        if step > 0:
-
-            @pl.when(low >= 0)
-            def _():
-                self.swap(low, chunk, self.half).start()
-
-            @pl.when(high < self.count)
-            def _():
-                self.hop(high, self.me + 1, step, self.send_left, chunk).wait_recv()
-
-        @pl.when(jnp.logical_and(high < self.count, self.has_left))
-        def _():
-            self.hop(high, self.me - 1, step, self.send_left, chunk).start()
-
-        if step > 0:
-
-            @pl.when(high < self.count)
-            def _():
-                self.swap(high, chunk, self.half).start()
+                self.hop(block, self.me + way, step, sems, chunk).start()
+
+            if chunk >= self.first_twin:
+                if step > 0:
+
+                    @pl.when(outer)
+                    def _():
+                        self.twin(block, self.me - way, step, chunk).wait_recv()
+
+                @pl.when(jnp.logical_and(outer, onward))
+                def _():
+                    self.twin(block, self.me + way, step, chunk).start()
+
+            if step > 0:
+                inner = jnp.logical_and(there, jnp.logical_not(outer))
+
+                @pl.when(inner if chunk >= self.first_twin else there)
+                def _():
+                    self.swap(block, chunk, self.half).start()
 
     def run(self, work):
         keep = pltpu.make_async_copy(self.own, self.out.at[self.me], self.local_sem)
@@ -153,26 +166,40 @@
         beyond = jnp.where(left < right, self.me + n - both, self.me - n + both)
         return jnp.where(n <= 2 * both, beside, beyond)
 
+    def swapped(self, block, chunk, act):
+        if chunk < self.first_twin:
+            act()
+        else:
+            pl.when(jnp.logical_and(block > 0, block < self.count - 1))(act)
+
     def arrive(self, block):
         for chunk in range(self.chunks):
-            self.swap(block, chunk, 1 - self.half).wait_recv()
+            self.swapped(block, chunk, lambda: self.swap(block, chunk, 1 - self.half).wait_recv())
 
     def drain(self):
         for step in range(self.count):
             low, high = self.me - step, self.me + step
+            ways = (
+                (low, low >= 0, low == 0, self.has_right, 1, self.send_right),
+                (high, high < self.count, high == self.count - 1, self.has_left, -1, self.send_left),
+            )
             for chunk in range(self.chunks):
-
-                @pl.when(jnp.logical_and(low >= 0, self.has_right))
-                def _():
-                    self.hop(low, self.me + 1, step, self.send_right, chunk).wait_send()
-
-                @pl.when(jnp.logical_and(high < self.count, self.has_left))
-                def _():
-                    self.hop(high, self.me - 1, step, self.send_left, chunk).wait_send()
+                for block, there, outer, onward, way, sems in ways:
+
+                    @pl.when(jnp.logical_and(there, onward))
+                    def _():
+                        self.hop(block, self.me + way, step, sems, chunk).wait_send()
+
+                    if chunk >= self.first_twin:
+
+                        @pl.when(jnp.logical_and(outer, onward))
+                        def _():
+                            self.twin(block, self.me + way, step, chunk).wait_send()
 
         for step in range(1, self.count):
+            block = lax.rem(self.me + step, self.count)
             for chunk in range(self.chunks):
-                self.swap(lax.rem(self.me + step, self.count), chunk, self.half).wait_send()
+                self.swapped(block, chunk, lambda: self.swap(block, chunk, self.half).wait_send())
 
 
 def prepare_sketch(pattern_ref, contrib, assembled, maps_ref, held):
@@ -318,39 +345,40 @@
                 self.scatter(r, phase).wait_send()
 
 
-def eliminate(leaves):
-    groups = NB // SUB
-    index = lax.broadcasted_iota(jnp.int32, (SUB, 2 * NB), 0)
-    wide = (SUB, 2 * NB)
-    leaves = [list(rows) for rows in leaves]
+def eliminate(rows, finish):
+    groups = len(rows)
+    wide = rows[0].shape
+    index = lax.broadcasted_iota(jnp.int32, wide, 0)
+    rows = list(rows)
     for panel in range(groups):
         first = panel * SUB
-        columns = [
-            {
-                q: [jnp.broadcast_to(rows[q][:, first + k : first + k + 1], wide) for k in range(SUB)]
-                for q in range(panel, groups)
-            }
-            for rows in leaves
-        ]
+        cols = {
+            q: [jnp.broadcast_to(rows[q][:, first + k : first + k + 1], wide) for k in range(SUB)]
+            for q in range(panel, groups)
+        }
+        own = cols[panel]
+        square = jnp.broadcast_to(own[0][0:1], wide)
         for k in range(SUB):
-            for rows, cols in zip(leaves, columns):
-                own = cols[panel]
-                scale = lax.rsqrt(jnp.broadcast_to(own[k][k : k + 1], wide))
-                pivot = jnp.broadcast_to(rows[panel][k : k + 1], wide) * scale
-                weight = {q: cols[q][k] * scale for q in range(panel, groups)}
-                across = weight[panel]
-                below = jnp.where(index > k, across, 0.0)
-                rows[panel] = jnp.where(index == k, pivot, rows[panel] - below * pivot)
-                for j in range(k + 1, SUB):
-                    factor = jnp.broadcast_to(across[j : j + 1], wide)
-                    for q in range(panel, groups):
-                        cols[q][j] = cols[q][j] - (below if q == panel else weight[q]) * factor
-                for q in range(panel + 1, groups):
-                    rows[q] = rows[q] - weight[q] * pivot
-    return leaves
-
-
-def factor(gram, work, done_block):
+            scale = lax.rsqrt(square)
+            if k + 1 < SUB:
+                beside = jnp.broadcast_to(own[k][k + 1 : k + 2], wide) * scale
+                square = jnp.broadcast_to(own[k + 1][k + 1 : k + 2], wide) - beside * beside
+            pivot = jnp.broadcast_to(rows[panel][k : k + 1], wide) * scale
+            weight = {q: cols[q][k] * scale for q in range(panel, groups)}
+            across = weight[panel]
+            below = jnp.where(index > k, across, 0.0)
+            rows[panel] = jnp.where(index == k, pivot, rows[panel] - below * pivot)
+            for j in range(k + 1, SUB):
+                factor = jnp.broadcast_to(across[j : j + 1], wide)
+                for q in range(panel, groups):
+                    cols[q][j] = cols[q][j] - (below if q == panel else weight[q]) * factor
+            for q in range(panel + 1, groups):
+                rows[q] = rows[q] - weight[q] * pivot
+        finish(panel, rows[panel])
+    return rows
+
+
+def factor(gram, work, upper, send):
     columns = gram.shape[0]
     eye = jnp.where(
         lax.broadcasted_iota(jnp.int32, (columns, columns), 0)
@@ -360,17 +388,35 @@
     )
     work[:, :columns] = gram
     work[:, columns:] = eye
-    small_eye = eye[:NB, :NB]
+    diagonal = gram[:NB, :NB]
     for block in range(columns // NB):
         begin, end = block * NB, (block + 1) * NB
-        diagonal = jnp.concatenate([work[begin:end, begin:end], small_eye], axis=1)
-        done = eliminate([[diagonal[q * SUB : (q + 1) * SUB] for q in range(NB // SUB)]])
-        inverse = jnp.concatenate(done[0], axis=0)[:, NB:]
-        rows = mm3(inverse, work[begin:end, :])
-        work[begin:end, :] = rows
-        done_block(block, begin, end, rows[:, :columns])
+        if begin > 0:
+            upper[begin:end, :begin] = jnp.zeros((NB, begin), jnp.float32)
+
+        def finish(panel, values):
+            start = panel * SUB
+            lane = lax.broadcasted_iota(jnp.int32, (SUB, NB), 1)
+            row = lax.broadcasted_iota(jnp.int32, (SUB, NB), 0) + start
+            upper[begin + start : begin + start + SUB, begin:end] = jnp.where(lane >= row, values[:, :NB], 0.0)
+            if end == columns and (start + SUB) % PIECE == 0:
+                send((begin + start) // PIECE).start()
+
+        both = jnp.concatenate([diagonal, eye[:NB, :NB]], axis=1)
+        done = eliminate([both[q * SUB : (q + 1) * SUB] for q in range(NB // SUB)], finish)
+        inverse = jnp.concatenate(done, axis=0)[:, NB:]
         if end < columns:
-            work[end:, :] = work[end:, :] - mm3(rows[:, end:columns], rows, TN)
+            right = mm3(inverse, work[begin:end, end:columns])
+            rest = work[end:, end:columns] - mm3(right, right, TN)
+            diagonal = rest[:NB, :NB]
+            work[end:, end:columns] = rest
+            upper[begin:end, end:] = right
+            for piece in range(begin // PIECE, end // PIECE):
+                send(piece).start()
+        left = mm3(inverse, work[begin:end, columns:])
+        work[begin:end, columns:] = left
+        if end < columns:
+            work[end:, columns:] = work[end:, columns:] - mm3(right, left, TN)
 
 
 def whole_kernel(
@@ -399,8 +445,8 @@
     greet(plane)
 
     row_count, row_pos = lax.axis_size("row"), lax.axis_index("row")
-    gather = Gather(omega_ref, gathered, sems[:6])
-    summing = Total(plane, part, sums, pair_buf, landed, window, sems[6:12])
+    gather = Gather(omega_ref, gathered, sems[:8])
+    summing = Total(plane, part, sums, pair_buf, landed, window, sems[8:14])
 
     def prepare():
         for copy in load_small + [load_front, load_entries]:
@@ -463,28 +509,21 @@
         summing.arrive(0)
         blocks = []
 
-    near_send, near_recv, end_send, end_recv = sems[12:]
+    near_send, near_recv, end_send, end_recv = sems[14:]
     near = {"row": row_pos + 1 - 2 * (row_pos % 2)}
 
-    def send(block):
-        start = block * NB // 128 * 128
-        rows = slice(block * NB, (block + 1) * NB)
+    def send(piece):
+        start = piece * PIECE // 128 * 128
+        rows = slice(piece * PIECE, (piece + 1) * PIECE)
         source, target = upper.at[rows, start:], sibling.at[rows, start:]
-        return remote(source, target, near_send.at[block], near_recv.at[block], near)
-
-    def done_block(block, begin, end, rows):
-        keep = lax.broadcasted_iota(jnp.int32, rows.shape, 1) >= begin + lax.broadcasted_iota(
-            jnp.int32, rows.shape, 0
-        )
-        upper[begin:end, :] = jnp.where(keep, rows, 0.0)
-        send(block).start()
+        return remote(source, target, near_send.at[piece], near_recv.at[piece], near)
 
     bound = bound_ref[...]
     samples = window[...].reshape(columns, span)
     place_of = lax.broadcasted_iota(jnp.int32, (columns, span), 1) + core * low
     masked = jnp.where((1 - 2 * core) * (bound - place_of) + core > 0, samples, 0.0)
     rows_of_leaf = (1 - core) * bound + core * (window_rows - bound)
-    factor(mm3(masked, masked, NT) / rows_of_leaf.astype(jnp.float32), work, done_block)
+    factor(mm3(masked, masked, NT) / rows_of_leaf.astype(jnp.float32), work, upper, send)
 
     pair_rows = pl.ds(pl.multiple_of(plane.chip * 2 * width, 2 * width), 2 * width)
     give_bases = remote(
@@ -496,11 +535,12 @@
     bases_out[...] = mm3(work[pair_rows, columns:], samples).reshape(bases_out.shape)
     give_bases.start()
     own = upper[pair_rows, :]
-    for block in range(columns // NB):
-        start = block * NB // 128 * 128
-        send(block).wait_recv()
-        piece = mm3(own[:, start:], sibling[block * NB : (block + 1) * NB, start:], NT)
-        coupling_out[:, :, block * NB : (block + 1) * NB] = piece.reshape(2, width, NB)
+    for piece in range(columns // PIECE):
+        start = piece * PIECE // 128 * 128
+        rows = slice(piece * PIECE, (piece + 1) * PIECE)
+        send(piece).wait_recv()
+        product = mm3(own[:, start:], sibling[rows, start:], NT)
+        coupling_out[:, :, rows] = product.reshape(2, width, PIECE)
     give_coupling.start()
     bases_in[core] = bases_out[core]
     coupling_ref[0, core] = coupling_out[core]
@@ -521,8 +561,8 @@
         summing.drain(block_of(n), double(n))
     if not blocks:
         summing.drain(0, True)
-    for block in range(columns // NB):
-        send(block).wait_send()
+    for piece in range(columns // PIECE):
+        send(piece).wait_send()
     give_bases.wait_send()
     give_coupling.wait_send()
 
@@ -580,12 +620,12 @@
             pltpu.VMEM((2, width, columns), f32),
             dma((4,)),
         ]
-        + [dma((rows, chunks))] * 5
+        + [dma((rows, chunks))] * 7
         + [dma]
         + [dma((stages,))] * 2
         + [dma((stages, max(phases, 3), 2))] * 2
         + [dma((stages,))] * 2
-        + [dma((columns // NB,))] * 2
+        + [dma((columns // PIECE,))] * 2
         + [dma((2,))] * 2,
         compiler_params=pltpu.CompilerParams(
             collective_id=0, has_side_effects=True, vmem_limit_bytes=(64 << 20) - ROOM

time: 51.2 us -> 48.8 us (0.953)
  Pallas kernels: 49.8 us -> 47.3 us
    pallas_call x1, Pallas kernels: 48.2 us -> 45.7 us  [local(): pl.pallas_call(whole_kernel, out_shape=(jax.ShapeDtypeStruct((width, wind...]
where the time goes in v3:
time: 48.8 us; the launch traced here: 48.6 us
  Pallas kernels  47.3 us (97%)
  between operations  1.29 us (3%)
    pallas_call x1, Pallas kernels, local(): pl.pallas_call(whole_kernel, out_shape=(jax.ShapeDtypeStruct((width, wind...  45.7 us
    pallas_call x1, Pallas kernels, local(): pl.pallas_call(deliver_kernel, out_shape=(jax.ShapeDtypeStruct(bases.shap...  1.59 us

profile of v3, /device:TPU:0, one launch (start us, length us, event | category | flops | bytes accessed | tf_op | source)
XLA Modules:
  0.0 48.6 jit_solution(4699056480316880542)
XLA Ops:
  1.3 45.7 %front_samples.1 = (f32[32,1024]{1,0:T(8,128)}, f32[1,2,32,256]{3,2,1,0:T(8,128)}) custom-call(s32[1,1]{1,0:T(1,128)} %bitcast.5.bound_ref, s32[4,4]{1,0:T(4,128)} %pattern_hbm.1, f32[2,32,1024]{2,1,0:T(8,128)} %bitcast.6, f32[1,512,512]{2,1,0:T(8,128)} %contrib_ref.1, f32[1,512,1024]{2,1,0:T(8,128)} %assembled_ref.1, s32[1,2048]{1,0:T(1,128)} %maps_hbm.1), custom_call_target="tpu_custom_call" | custom-call | tf_op jit(solution)/shard_map/front_samples/pallas_call | solution.py:591
  47.0 1.6 %deliver.1 = (f32[32,1024]{1,0:T(8,128)}, f32[1,2,32,256]{3,2,1,0:T(8,128)}) custom-call(f32[32,1024]{1,0:T(8,128)} %get-tuple-element.6.bases_ref, f32[1,2,32,256]{3,2,1,0:T(8,128)} %get-tuple-element.7.coupling_ref), custom_call_target="tpu_custom_call" | custom-call | tf_op jit(solution)/shard_map/deliver/pallas_call | solution.py:635

commit v4 on v3

--- a/solution.py
+++ b/solution.py
@@ -11,6 +11,8 @@
 SUB = 8
 CHUNK = 8
 TWINS = 1
+EARLY = ((1, 2, 0), (2, 3, 0), (3, 0, 11))
+LATE = (1, 12, 0, 1, 2, 13, 0, 1, 2, 3)
 ROOM = 8 << 20
 SMALL = 62 << 20
 DOUBLED = 1
@@ -423,12 +425,12 @@
     bound_ref, pattern_hbm, omega_ref, contrib_ref, assembled_ref, maps_hbm, bases_ref, coupling_ref,
     pattern_ref, maps_ref, gathered, contrib_buf, assembled_buf, pick, place, front, entries,
     part, sums, pair_buf, landed, window, work, upper, sibling, bases_out, bases_in, coupling_out, coupling_in,
-    input_sems, *sems,
+    bases_buf, input_sems, *sems,
 ):
     plane = Plane()
     core = plane.core
     window_rows = assembled_buf.shape[1]
-    columns, width = upper.shape[1], bases_ref.shape[0]
+    columns, width = upper.shape[1], bases_buf.shape[0]
     stages, span = window.shape[0], window.shape[2]
     low = window_rows - span
     held = (pick, place, front, entries)
@@ -484,20 +486,24 @@
 
         end, mid = gather.chunks - 1, gather.chunks // 2
         queue = {(0, end): [prepare, lambda: begin(0)]}
-        queue.setdefault((1, mid), []).append(lambda: go(0))
-        queue.setdefault((2, end), []).append(lambda: go(0))
-        if row_count > 3:
-            queue.setdefault((3, 0), []).append(lambda: begin(1))
+        for step, chunk, n in EARLY:
+            if step < row_count:
+                queue.setdefault((step, min(chunk, end)), []).append(
+                    (lambda n=n: begin(n - 10)) if n >= 10 else (lambda n=n: go(n))
+                )
         gather.run(queue)
-        go(1)
+        for n in LATE:
+            if n >= 10 and 10 + len(begun) <= n < 10 + stages:
+                begin(n - 10)
+            elif n < 10:
+                go(n)
         for n in range(len(begun), stages):
             begin(n)
             go_all()
         while any(left.values()):
             go_all()
         blocks = range(stages)
-        for n in blocks:
-            summing.arrive(block_of(n))
+        landing = [block_of(n) for n in blocks]
     else:
         gather.run({(0, 0): [prepare]})
         for step in range(1, row_count):
@@ -506,8 +512,7 @@
         summing.begin(0)
         for phase in range(summing.steps(True)):
             summing.advance(0, phase, True)
-        summing.arrive(0)
-        blocks = []
+        blocks, landing = [], [0]
 
     near_send, near_recv, end_send, end_recv = sems[14:]
     near = {"row": row_pos + 1 - 2 * (row_pos % 2)}
@@ -519,11 +524,21 @@
         return remote(source, target, near_send.at[piece], near_recv.at[piece], near)
 
     bound = bound_ref[...]
+    rows_of_leaf = (1 - core) * bound + core * (window_rows - bound)
+
+    def leaf_gram(lanes, first):
+        values = window[:, :, lanes].reshape(columns, lanes.size)
+        place_of = lax.broadcasted_iota(jnp.int32, values.shape, 1) + first
+        masked = jnp.where((1 - 2 * core) * (bound - place_of) + core > 0, values, 0.0)
+        return mm3(masked, masked, NT)
+
+    half, shared = summing.half, summing.shared
+    gram = leaf_gram(summing.place, core * half)
+    for block in landing:
+        summing.arrive(block)
+    gram = gram + leaf_gram(summing.lanes((1 - core) * half, shared), core * low + (1 - core) * half)
+    factor(gram / rows_of_leaf.astype(jnp.float32), work, upper, send)
     samples = window[...].reshape(columns, span)
-    place_of = lax.broadcasted_iota(jnp.int32, (columns, span), 1) + core * low
-    masked = jnp.where((1 - 2 * core) * (bound - place_of) + core > 0, samples, 0.0)
-    rows_of_leaf = (1 - core) * bound + core * (window_rows - bound)
-    factor(mm3(masked, masked, NT) / rows_of_leaf.astype(jnp.float32), work, upper, send)
 
     pair_rows = pl.ds(pl.multiple_of(plane.chip * 2 * width, 2 * width), 2 * width)
     give_bases = remote(
@@ -534,27 +549,37 @@
     )
     bases_out[...] = mm3(work[pair_rows, columns:], samples).reshape(bases_out.shape)
     give_bases.start()
+    bases_in[core] = bases_out[core]
     own = upper[pair_rows, :]
-    for piece in range(columns // PIECE):
+    finished = []
+
+    def finish(source, target):
+        copy = pltpu.make_async_copy(source, target, input_sems.at[len(finished)])
+        copy.start()
+        finished.append(copy)
+
+    pieces = columns // PIECE
+    for piece in range(pieces):
+        if piece == pieces // 2:
+            remote(
+                bases_out.at[core], bases_in.at[1 - core], end_send.at[0], end_recv.at[0], plane.partner
+            ).wait_recv()
+            bases_buf[:, :low] = bases_in[0, :, :low]
+            bases_buf[:, span:] = bases_in[1, :, span - low :]
+            lane = lax.broadcasted_iota(jnp.int32, (width, span - low), 1) + low
+            bases_buf[:, low:span] = jnp.where(lane < bound, bases_in[0, :, low:], bases_in[1, :, : span - low])
+            finish(bases_buf, bases_ref)
         start = piece * PIECE // 128 * 128
         rows = slice(piece * PIECE, (piece + 1) * PIECE)
         send(piece).wait_recv()
         product = mm3(own[:, start:], sibling[rows, start:], NT)
         coupling_out[:, :, rows] = product.reshape(2, width, PIECE)
     give_coupling.start()
-    bases_in[core] = bases_out[core]
-    coupling_ref[0, core] = coupling_out[core]
-    remote(
-        bases_out.at[core], bases_in.at[1 - core], end_send.at[0], end_recv.at[0], plane.partner
-    ).wait_recv()
-    bases_ref[:, :low] = bases_in[0, :, :low]
-    bases_ref[:, span:] = bases_in[1, :, span - low :]
-    lane = lax.broadcasted_iota(jnp.int32, (width, span - low), 1) + low
-    bases_ref[:, low:span] = jnp.where(lane < bound, bases_in[0, :, low:], bases_in[1, :, : span - low])
+    finish(coupling_out.at[core], coupling_ref.at[0, core])
     remote(
         coupling_out.at[core], coupling_in.at[1 - core], end_send.at[1], end_recv.at[1], plane.partner
     ).wait_recv()
-    coupling_ref[0, 1 - core] = coupling_in[1 - core]
+    finish(coupling_in.at[1 - core], coupling_ref.at[0, 1 - core])
 
     gather.drain()
     for n in blocks:
@@ -565,6 +590,8 @@
         send(piece).wait_send()
     give_bases.wait_send()
     give_coupling.wait_send()
+    for copy in finished:
+        copy.wait()
 
 
 def deliver_kernel(bases_ref, coupling_ref, bases_out, coupling_out):
@@ -595,7 +622,7 @@
             jax.ShapeDtypeStruct((1, 2, width, columns), f32),
         ),
         in_specs=[VMEM] + [any_space] * 5,
-        out_specs=(VMEM, VMEM),
+        out_specs=(any_space, any_space),
         scratch_shapes=[
             pltpu.SMEM(pattern.shape, jnp.int32),
             pltpu.VMEM(row_maps.shape, jnp.int32),
@@ -618,6 +645,7 @@
             pltpu.VMEM((2, width, span), f32),
             pltpu.VMEM((2, width, columns), f32),
             pltpu.VMEM((2, width, columns), f32),
+            pltpu.VMEM((width, window_rows), f32),
             dma((4,)),
         ]
         + [dma((rows, chunks))] * 7

time: 48.8 us -> 48.7 us (level)
  no operation moved by 1% of the time
where the time goes in v4:
time: 48.7 us; the launch traced here: 48.5 us
  Pallas kernels  47.2 us (97%)
  between operations  1.29 us (3%)
    pallas_call x1, Pallas kernels, local(): pl.pallas_call(whole_kernel, out_shape=(jax.ShapeDtypeStruct((width, wind...  45.6 us
    pallas_call x1, Pallas kernels, local(): pl.pallas_call(deliver_kernel, out_shape=(jax.ShapeDtypeStruct(bases.shap...  1.59 us

profile of v4, /device:TPU:0, one launch (start us, length us, event | category | flops | bytes accessed | tf_op | source)
XLA Modules:
  0.0 48.5 jit_solution(8741562199025619208)
XLA Ops:
  1.3 45.6 %front_samples.1 = (f32[32,1024]{1,0:T(8,128)}, f32[1,2,32,256]{3,2,1,0:T(8,128)}) custom-call(s32[1,1]{1,0:T(1,128)} %bitcast.5.bound_ref, s32[4,4]{1,0:T(4,128)} %pattern_hbm.1, f32[2,32,1024]{2,1,0:T(8,128)} %bitcast.6, f32[1,512,512]{2,1,0:T(8,128)} %contrib_ref.1, f32[1,512,1024]{2,1,0:T(8,128)} %assembled_ref.1, s32[1,2048]{1,0:T(1,128)} %maps_hbm.1), custom_call_target="tpu_custom_call" | custom-call | tf_op jit(solution)/shard_map/front_samples/pallas_call | solution.py:618
  46.9 1.6 %deliver.1 = (f32[32,1024]{1,0:T(8,128)}, f32[1,2,32,256]{3,2,1,0:T(8,128)}) custom-call(f32[32,1024]{1,0:T(8,128)} %get-tuple-element.6.bases_ref, f32[1,2,32,256]{3,2,1,0:T(8,128)} %get-tuple-element.7.coupling_ref), custom_call_target="tpu_custom_call" | custom-call | tf_op jit(solution)/shard_map/deliver/pallas_call | solution.py:663
